TPU v7x, 128 devices: a whole 4x4x4 slice. The times are simulated.
128 devices in a mesh: seq: 32 (over y, x, z_lo), head: 4 (over z_hi, core).
Axes of the slice: x: 4, y: 4, z: 4 (z_hi: 2, z_lo: 2; z = z_hi * 2 + z_lo), core: 2. Of those that a mesh axis runs over, the one named last changes fastest.
Arguments:
- queries: bfloat16 [8192, 2048], P('seq', 'head'), may hold values from -24 to 24
- key_vectors: bfloat16 [8192, 512], P('seq', 'head'), may hold values from -4 to 4
- values: bfloat16 [8192, 512], P('seq', 'head'), may hold values from -6 to 6
- out_proj: bfloat16 [2048, 4096], P('head'), may hold values from -0.125 to 0.125
- grad_out: bfloat16 [8192, 4096], P('seq', 'head'), may hold values from -6 to 6
- windows: int32 [16], P('head'), may hold values from 1024 to 2048, as said below
- slab_order: int32 [32], replicated, may hold values from 0 to 31, as said below
Outputs:
- layer_out: bfloat16 [8192, 4096], P('seq', 'head')
- grad_queries: bfloat16 [8192, 2048], P('seq', 'head')
- grad_keys: bfloat16 [8192, 512], P('seq', 'head')
- grad_values: bfloat16 [8192, 512], P('seq', 'head')
Inputs may be any that keep to these rules, and one draw needn't show every extreme that they name: `windows`: some head's window is exactly 2048. slab_order[d] = (d + c) mod 32 for one c with 0 <= c < 32.
All inputs are finite; a program needn't handle non-finite values.
Results may differ from a plain program's by a relative error of at most 0.019.
Values may be sent and summed in bfloat16 or wider, within the bound.
A program may use at most 128 MiB of HBM per device.

v0:
```python
import jax
import jax.numpy as jnp
from jax import lax
from jax.experimental import pallas as pl
from jax.experimental.pallas import tpu as pltpu
from jax.sharding import PartitionSpec as P

MESH = pl.DeviceIdType.MESH
BF = jnp.bfloat16
F32 = jnp.float32
ROWS = 256
DIM = 128
RATIO = 4
SCALE = DIM ** (-0.5)
LOWEST = -1e30
OWN, SPARE = 8, 9


def nn(a, b):
    return jnp.dot(a, b, preferred_element_type=F32)


def nt(a, b):
    return lax.dot_general(a, b, (((1,), (1,)), ((), ())), preferred_element_type=F32)


def kernel(
    order, spans, q_hbm, k_hbm, v_hbm, w_hbm, g_hbm,
    out_ref, gq_ref, gk_ref, gv_ref,
    qv, kv, w, gb, qt, qs, st, peak, total, acc, gsum, dos, dot_t, lse, delta, dqt, attn,
    sh_send, sh_f0, sh_part, sh_opp, dsend, drecv, ysend, yrecv, dacc, place,
    lsem, c_send, c_recv, a_send, a_recv, b_send, b_recv, d_send, d_recv,
):
    s = lax.axis_index("seq")
    hd = lax.axis_index("head")
    y, x, zl = s // 8, (s // 2) % 4, s % 2
    zh, core = hd // 2, hd % 2
    r = 2 * x + zl
    rp = 2 * x + 1 - zl
    row0 = y * 8
    up = ((y + 1) % 4) * 8
    down = ((y + 3) % 4) * 8
    partner = {"head": 2 * zh + 1 - core}
    opposite = {"head": 2 * (1 - zh) + core}
    q0, q1 = 2 * zh + core, 2 * zh + 1 - core
    f0, f1 = 2 * (1 - zh) + core, 2 * (1 - zh) + 1 - core

    def at_seq(index):
        return {"seq": index}

    def remote(src, dst, send, recv, device):
        return pltpu.make_async_remote_copy(
            src_ref=src, dst_ref=dst, send_sem=send, recv_sem=recv, device_id=device, device_id_type=MESH
        )

    loads = [
        pltpu.make_async_copy(k_hbm, kv.at[OWN, pl.ds(0, ROWS)], lsem.at[0]),
        pltpu.make_async_copy(v_hbm, kv.at[OWN, pl.ds(ROWS, ROWS)], lsem.at[1]),
        pltpu.make_async_copy(g_hbm, gb.at[0], lsem.at[2]),
        pltpu.make_async_copy(q_hbm, qv, lsem.at[3]),
        pltpu.make_async_copy(w_hbm, w, lsem.at[4]),
    ]
    for load in loads:
        load.start()

    barrier = pltpu.get_barrier_semaphore()
    for away in range(1, 8):
        pl.semaphore_signal(barrier, inc=1, device_id=at_seq(row0 + (r + away) % 8), device_id_type=MESH)
    for device in (partner, opposite, at_seq(up + r), at_seq(down + r)):
        pl.semaphore_signal(barrier, inc=1, device_id=device, device_id_type=MESH)
    pl.semaphore_wait(barrier, 11)

    op_slot = jnp.where(zl == 0, SPARE, r - 1)
    yp_slot = jnp.where(zl == 0, r + 1, SPARE)
    op_there = jnp.where(zl == 1, SPARE, r)

    def kv_copy(src, dst, send, device):
        return remote(kv.at[src], kv.at[dst], c_send.at[send], c_recv.at[dst], device)

    def side(away, other):
        xx = (x + away) % 4
        later = xx > x
        if other:
            src = jnp.where(later, op_slot, yp_slot)
        else:
            src = jnp.where(later, OWN, r)
        dst = rp if other else r
        return later, kv_copy(src, dst, 3 + 2 * (away - 1) + other, at_seq(row0 + 2 * xx + zl))

    def start_sides(other, later_now):
        for away in (2, 1, 3):
            later, copy = side(away, other)

            @pl.when(later if later_now else jnp.logical_not(later))
            def _():
                copy.start()

    loads[0].wait()
    loads[1].wait()
    to_half = kv_copy(OWN, op_there, 0, at_seq(row0 + rp))
    to_half.start()
    to_up = kv_copy(OWN, r, 1, at_seq(up + r))
    to_up.start()
    start_sides(0, True)
    loads[2].wait()
    half = ROWS // 2
    a_opp = [
        remote(gb.at[0, pl.ds(i * half, half)], gb.at[2, pl.ds(i * half, half)], a_send.at[i], a_recv.at[i], opposite)
        for i in range(2)
    ]
    a_part = remote(gb.at[0], gb.at[1], a_send.at[2], a_recv.at[2], partner)
    a_fwd = [
        remote(gb.at[2, pl.ds(i * half, half)], gb.at[3, pl.ds(i * half, half)], a_send.at[3 + i], a_recv.at[3 + i], partner)
        for i in range(2)
    ]
    a_part.start()
    for copy in a_opp:
        copy.start()

    loads[3].wait()
    for h in range(RATIO):
        block = qv[:, h * DIM : (h + 1) * DIM]
        qs[pl.ds(h * ROWS, ROWS), :] = block
        qt[:, h * ROWS : (h + 1) * ROWS] = block.T
    place[...] = lax.broadcasted_iota(jnp.int32, (ROWS, ROWS), 1) - lax.broadcasted_iota(jnp.int32, (ROWS, ROWS), 0)

    mine = order[s]

    def forward(j, slot, hidden):
        key = kv[slot, pl.ds(0, ROWS), :]
        value_t = kv[slot, pl.ds(ROWS, ROWS), :].T
        for h in range(RATIO):
            cols = slice(h * ROWS, (h + 1) * ROWS)
            scores = jnp.where(hidden(h), LOWEST, nn(key, qt[:, cols]) * SCALE)
            st[j, :, cols] = scores
            top = jnp.max(scores, axis=0, keepdims=True)
            if hidden is causal:
                probs = jnp.exp(scores - top)
                peak[:, cols] = top
                total[:, cols] = jnp.sum(probs, axis=0, keepdims=True)
                acc[:, cols] = nn(value_t, probs.astype(BF))
            else:
                before = peak[:, cols]
                top = jnp.maximum(before, top)
                fade = jnp.exp(before - top)
                probs = jnp.exp(scores - top)
                peak[:, cols] = top
                total[:, cols] = total[:, cols] * fade + jnp.sum(probs, axis=0, keepdims=True)
                acc[:, cols] = acc[:, cols] * fade + nn(value_t, probs.astype(BF))

    def causal(h):
        return place[...] < 0

    def slot_of(j):
        pair = jnp.maximum(j - 3, 0) // 2
        away = 1 + 2 * pair - 3 * (pair // 2)
        parity = (zl + (j - 3) % 2) % 2
        return jnp.where(j == 1, rp, jnp.where(j == 2, r, 2 * ((x + away) % 4) + parity))

    def row_of(slot):
        return jnp.where(slot < r, row0, down)

    forward(0, OWN, causal)

    def await_slot(slot):
        kv_copy(OWN, slot, 0, at_seq(row0 + rp)).wait_recv()

    await_slot(op_slot)
    op_up = kv_copy(op_slot, yp_slot, 2, at_seq(up + r))
    op_up.start()
    start_sides(1, True)
    await_slot(r)
    start_sides(0, False)

    loads[4].wait()

    def w_cols(quarter):
        return pl.ds(pl.multiple_of(quarter * 1024, 1024), 1024)

    gsum[...] = nt(gb[0], w[:, w_cols(q0)])
    a_part.wait_recv()
    gsum[...] += nt(gb[1], w[:, w_cols(q1)])

    await_slot(yp_slot)
    start_sides(1, False)

    def forward_step(j, carry):
        slot = slot_of(j)

        @pl.when(j >= 3)
        def _():
            await_slot(slot)

        gap = (mine - order[row_of(slot) + slot]) * ROWS

        def windowed(h):
            limit = jnp.where(gap > 0, spans[h] - gap, -100000)
            return place[...] >= limit

        forward(j, slot, windowed)
        return carry

    lax.fori_loop(1, 9, forward_step, 0)

    for i in range(2):
        a_opp[i].wait_recv()
        a_fwd[i].start()

    norm = 1.0 / total[...]
    lse[...] = peak[...] + jnp.log(total[...])
    for h in range(RATIO):
        cols = slice(h * ROWS, (h + 1) * ROWS)
        mixed = (acc[:, cols] * norm[:, cols]).astype(BF)
        attn[:, h * DIM : (h + 1) * DIM] = mixed.T
        acc[:, cols] = mixed.astype(F32)

    def share(quarter):
        return nn(attn[...], w[:, w_cols(quarter)])

    sh_send[0] = share(f1).astype(BF)
    b_part = [remote(sh_send.at[i], sh_part.at[i], b_send.at[i], b_recv.at[i], partner) for i in range(2)]
    b_part[0].start()

    gsum[...] += nt(gb[2], w[:, w_cols(f0)])
    b_part[0].wait_recv()
    sh_f0[...] = (share(f0) + sh_part[0].astype(F32)).astype(BF)
    b_opp = remote(sh_f0, sh_opp, b_send.at[2], b_recv.at[2], opposite)
    b_opp.start()
    for copy in a_fwd:
        copy.wait_recv()
    gsum[...] += nt(gb[3], w[:, w_cols(f1)])
    for h in range(RATIO):
        cols = slice(h * ROWS, (h + 1) * ROWS)
        grad = gsum[:, h * DIM : (h + 1) * DIM].astype(BF)
        dos[pl.ds(h * ROWS, ROWS), :] = grad
        grad_t = grad.T
        dot_t[:, cols] = grad_t
        delta[:, cols] = jnp.sum(grad_t.astype(F32) * acc[:, cols], axis=0, keepdims=True)

    def backward(j, slot):
        key_t = kv[slot, pl.ds(0, ROWS), :].T
        value = kv[slot, pl.ds(ROWS, ROWS), :]
        probs_all = []
        grads_all = []
        for h in range(RATIO):
            cols = slice(h * ROWS, (h + 1) * ROWS)
            probs = jnp.exp(st[j, :, cols] - lse[:, cols])
            grad_probs = nn(value, dot_t[:, cols])
            probs_all.append(probs.astype(BF))
            grads_all.append((probs * (grad_probs - delta[:, cols])).astype(BF))
        probs_all = jnp.concatenate(probs_all, axis=1)
        grads_all = jnp.concatenate(grads_all, axis=1)
        grad_key = nn(grads_all, qs[...]) * SCALE
        grad_value = nn(probs_all, dos[...])
        dqt[...] += nn(key_t, grads_all)
        return grad_key, grad_value

    dqt[...] = jnp.zeros_like(dqt)

    def kv_grad_copy(slot):
        return remote(dsend.at[slot], drecv.at[r], d_send.at[slot], d_recv.at[r], at_seq(row0 + slot))

    def backward_step(i, carry):
        j = 8 - i
        slot = slot_of(j)
        grad_key, grad_value = backward(j, slot)

        @pl.when(j != 2)
        def _():
            dsend[slot, pl.ds(0, ROWS), :] = grad_key.astype(BF)
            dsend[slot, pl.ds(ROWS, ROWS), :] = grad_value.astype(BF)
            kv_grad_copy(slot).start()

        @pl.when(j == 2)
        def _():
            dacc[1, pl.ds(0, ROWS), :] = grad_key
            dacc[1, pl.ds(ROWS, ROWS), :] = grad_value

        return carry

    lax.fori_loop(0, 8, backward_step, 0)
    grad_key, grad_value = backward(0, OWN)
    dacc[0, pl.ds(0, ROWS), :] = grad_key
    dacc[0, pl.ds(ROWS, ROWS), :] = grad_value

    sh_send[1] = share(q1).astype(BF)
    b_part[1].start()
    for h in range(RATIO):
        gq_ref[:, h * DIM : (h + 1) * DIM] = (dqt[:, h * ROWS : (h + 1) * ROWS] * SCALE).astype(BF).T
    whole = share(q0)

    def add_from(index, which):
        remote(dsend.at[index], drecv.at[index], d_send.at[index], d_recv.at[index], at_seq(row0 + rp)).wait_recv()
        dacc[which] += drecv[index].astype(F32)

    @pl.loop(0, r)
    def _(index):
        add_from(index, 1)

    ysend[...] = dacc[1].astype(BF)
    y_copy = remote(ysend, yrecv, d_send.at[8], d_recv.at[8], at_seq(down + r))
    y_copy.start()

    @pl.loop(r + 1, 8)
    def _(index):
        add_from(index, 0)

    b_part[1].wait_recv()
    b_opp.wait_recv()
    out_ref[...] = (whole + sh_part[1].astype(F32) + sh_opp[...].astype(F32)).astype(BF)

    y_copy.wait_recv()
    final = dacc[0] + yrecv[...].astype(F32)
    gk_ref[...] = final[:ROWS].astype(BF)
    gv_ref[...] = final[ROWS:].astype(BF)

    for copy in (to_half, to_up, op_up, a_part, *a_opp, *a_fwd, *b_part, b_opp, y_copy):
        copy.wait_send()
    for away in (1, 2, 3):
        for other in (0, 1):
            side(away, other)[1].wait_send()
    for away in range(1, 8):
        kv_grad_copy((r + away) % 8).wait_send()


def body(queries, key_vectors, values, out_proj, grad_out, windows, slab_order):
    hbm = pl.BlockSpec(memory_space=pl.ANY)
    smem = pl.BlockSpec(memory_space=pltpu.SMEM)
    vmem = pl.BlockSpec(memory_space=pltpu.VMEM)
    wide = RATIO * ROWS
    return pl.pallas_call(
        kernel,
        name="layer",
        out_shape=(
            jax.ShapeDtypeStruct((ROWS, 1024), BF),
            jax.ShapeDtypeStruct((ROWS, RATIO * DIM), BF),
            jax.ShapeDtypeStruct((ROWS, DIM), BF),
            jax.ShapeDtypeStruct((ROWS, DIM), BF),
        ),
        in_specs=[smem, smem, hbm, hbm, hbm, hbm, hbm],
        out_specs=(vmem, vmem, vmem, vmem),
        scratch_shapes=[
            pltpu.VMEM((ROWS, RATIO * DIM), BF),
            pltpu.VMEM((10, 2 * ROWS, DIM), BF),
            pltpu.VMEM((RATIO * DIM, 4096), BF),
            pltpu.VMEM((4, ROWS, 1024), BF),
            pltpu.VMEM((DIM, wide), BF),
            pltpu.VMEM((wide, DIM), BF),
            pltpu.VMEM((9, ROWS, wide), F32),
            pltpu.VMEM((1, wide), F32),
            pltpu.VMEM((1, wide), F32),
            pltpu.VMEM((DIM, wide), F32),
            pltpu.VMEM((ROWS, RATIO * DIM), F32),
            pltpu.VMEM((wide, DIM), BF),
            pltpu.VMEM((DIM, wide), BF),
            pltpu.VMEM((1, wide), F32),
            pltpu.VMEM((1, wide), F32),
            pltpu.VMEM((DIM, wide), F32),
            pltpu.VMEM((ROWS, RATIO * DIM), BF),
            pltpu.VMEM((2, ROWS, 1024), BF),
            pltpu.VMEM((ROWS, 1024), BF),
            pltpu.VMEM((2, ROWS, 1024), BF),
            pltpu.VMEM((ROWS, 1024), BF),
            pltpu.VMEM((8, 2 * ROWS, DIM), BF),
            pltpu.VMEM((8, 2 * ROWS, DIM), BF),
            pltpu.VMEM((2 * ROWS, DIM), BF),
            pltpu.VMEM((2 * ROWS, DIM), BF),
            pltpu.VMEM((2, 2 * ROWS, DIM), F32),
            pltpu.VMEM((ROWS, ROWS), jnp.int32),
            pltpu.SemaphoreType.DMA((5,)),
            pltpu.SemaphoreType.DMA((9,)),
            pltpu.SemaphoreType.DMA((10,)),
            pltpu.SemaphoreType.DMA((5,)),
            pltpu.SemaphoreType.DMA((5,)),
            pltpu.SemaphoreType.DMA((3,)),
            pltpu.SemaphoreType.DMA((3,)),
            pltpu.SemaphoreType.DMA((9,)),
            pltpu.SemaphoreType.DMA((9,)),
        ],
        compiler_params=pltpu.CompilerParams(collective_id=0, has_side_effects=True, vmem_limit_bytes=56 * 1024 * 1024),
    )(slab_order, windows, queries, key_vectors, values, out_proj, grad_out)


def solution(mesh):
    in_specs = (
        P("seq", "head"),
        P("seq", "head"),
        P("seq", "head"),
        P("head", None),
        P("seq", "head"),
        P("head"),
        P(),
    )
    out_specs = (P("seq", "head"), P("seq", "head"), P("seq", "head"), P("seq", "head"))
    return jax.shard_map(body, mesh=mesh, in_specs=in_specs, out_specs=out_specs, check_vma=False)
```

profile of v0, /device:TPU:56, one launch (start us, length us, event | category | flops | bytes accessed | tf_op | source)
XLA Modules:
  0.0 67.6 jit_solution(13565559980252414593)
XLA Ops:
  0.6 60.4 %layer.1 = (bf16[256,1024]{1,0:T(8,128)(2,1)}, bf16[256,512]{1,0:T(8,128)(2,1)}, bf16[256,128]{1,0:T(8,128)(2,1)}, bf16[256,128]{1,0:T(8,128)(2,1)}) custom-call(s32[32]{0:T(128)} %order.1, s32[4]{0:T(128)} %spans.1, bf16[256,512]{1,0:T(8,128)(2,1)} %q_hbm.1, bf16[256,128]{1,0:T(8,128)(2,1)} %k_hbm.1, bf16[256,128]{1,0:T(8,128)(2,1)} %v_hbm.1, ...), custom_call_target="tpu_custom_call" | custom-call | tf_op jit(solution)/shard_map/layer/pallas_call | solution.py:331
  61.1 1.9 %copy.15 = bf16[256,1024]{1,0:T(8,128)(2,1)} copy(bf16[256,1024]{1,0:T(8,128)(2,1)} %get-tuple-element.8) | data formatting | bytes 1048576
  62.9 1.7 %copy.16 = bf16[256,512]{1,0:T(8,128)(2,1)} copy(bf16[256,512]{1,0:T(8,128)(2,1)} %get-tuple-element.9) | data formatting | bytes 524288
  64.6 1.5 %copy.17 = bf16[256,128]{1,0:T(8,128)(2,1)} copy(bf16[256,128]{1,0:T(8,128)(2,1)} %get-tuple-element.10) | data formatting | bytes 131072
  66.1 1.5 %copy.18 = bf16[256,128]{1,0:T(8,128)(2,1)} copy(bf16[256,128]{1,0:T(8,128)(2,1)} %get-tuple-element.11) | data formatting | bytes 131072
where the time goes:
time: 67.8 us; the launch traced here: 67.6 us
  Pallas kernels  60.4 us (89%)
  local copies, waits for them, and re-layouts  6.48 us (10%)
    pallas_call x1, Pallas kernels, body(): pl.pallas_call(kernel, name='layer', out_shape=(jax.ShapeDtypeStruct((ROW...  60.4 us
    unnamed x4, local copies, waits for them, and re-layouts  6.48 us

commit v1 on v0

v1 whole, which is shorter than its diff:
```python
import jax
import jax.numpy as jnp
from jax import lax
from jax.experimental import pallas as pl
from jax.experimental.pallas import tpu as pltpu
from jax.sharding import PartitionSpec as P

MESH = pl.DeviceIdType.MESH
BF = jnp.bfloat16
F32 = jnp.float32
ROWS = 256
DIM = 128
RATIO = 4
SCALE = DIM ** (-0.5)
LOG2E = 1.4426950408889634
LOWEST = -1e30
OWN, SPARE = 8, 9


def nn(a, b):
    return jnp.dot(a, b, preferred_element_type=F32)


def nt(a, b):
    return lax.dot_general(a, b, (((1,), (1,)), ((), ())), preferred_element_type=F32)


def kernel(
    order, spans, q_hbm, k_hbm, v_hbm, w_hbm, g_hbm,
    out_ref, gq_ref, gk_ref, gv_ref,
    qv, kv, w, gb, qt, qs, st, peak, total, acc, gsum, dos, dot_t, lse, delta, dqt, attn,
    sh_send, sh_f0, sh_part, sh_opp, dsend, drecv, ysend, yrecv, zsend, zrecv, dacc, place,
    lsem, c_send, c_recv, a_send, a_recv, b_send, b_recv, d_send, d_recv, y_send, y_recv, z_send, z_recv,
):
    s = lax.axis_index("seq")
    hd = lax.axis_index("head")
    y, x, zl = s // 8, (s // 2) % 4, s % 2
    zh, core = hd // 2, hd % 2
    r = 2 * x + zl
    rp = 2 * x + 1 - zl
    row0 = y * 8
    up = ((y + 1) % 4) * 8
    down = ((y + 3) % 4) * 8
    partner = {"head": 2 * zh + 1 - core}
    opposite = {"head": 2 * (1 - zh) + core}
    q0, q1 = 2 * zh + core, 2 * zh + 1 - core
    f0, f1 = 2 * (1 - zh) + core, 2 * (1 - zh) + 1 - core

    def at_seq(index):
        return {"seq": index}

    def remote(src, dst, send, recv, device):
        return pltpu.make_async_remote_copy(
            src_ref=src, dst_ref=dst, send_sem=send, recv_sem=recv, device_id=device, device_id_type=MESH
        )

    loads = [
        pltpu.make_async_copy(k_hbm, kv.at[OWN, 0], lsem.at[0]),
        pltpu.make_async_copy(v_hbm, kv.at[OWN, 1], lsem.at[1]),
        pltpu.make_async_copy(g_hbm, gb.at[0], lsem.at[2]),
        pltpu.make_async_copy(q_hbm, qv, lsem.at[3]),
        pltpu.make_async_copy(w_hbm, w, lsem.at[4]),
    ]
    for load in loads:
        load.start()

    barrier = pltpu.get_barrier_semaphore()
    for away in range(1, 4):
        pl.semaphore_signal(barrier, inc=1, device_id=at_seq(row0 + (r + 2 * away) % 8), device_id_type=MESH)
    for device in (at_seq(row0 + rp), partner, opposite, at_seq(up + r), at_seq(down + r)):
        pl.semaphore_signal(barrier, inc=1, device_id=device, device_id_type=MESH)
    place[...] = lax.broadcasted_iota(jnp.int32, (ROWS, ROWS), 1) - lax.broadcasted_iota(jnp.int32, (ROWS, ROWS), 0)
    dqt[...] = jnp.zeros_like(dqt)
    dacc[zl, 1] = jnp.zeros((2, ROWS, DIM), F32)
    loads[3].wait()
    for h in range(RATIO):
        block = qv[:, h * DIM : (h + 1) * DIM]
        qs[pl.ds(h * ROWS, ROWS), :] = block
        qt[:, h * ROWS : (h + 1) * ROWS] = block.T
    for i in range(3):
        loads[i].wait()
    pl.semaphore_wait(barrier, 8)

    op_slot = jnp.where(zl == 0, SPARE, r - 1)
    yp_slot = jnp.where(zl == 0, r + 1, SPARE)
    op_there = jnp.where(zl == 1, SPARE, r)

    def kv_copy(src, dst, part, send, device):
        return remote(kv.at[src, part], kv.at[dst, part], c_send.at[send, part], c_recv.at[dst, part], device)

    def side(away, other, part):
        xx = (x + away) % 4
        later = xx > x
        if other:
            src = jnp.where(later, op_slot, yp_slot)
        else:
            src = jnp.where(later, OWN, r)
        dst = rp if other else r
        return later, kv_copy(src, dst, part, 3 + 2 * (away - 1) + other, at_seq(row0 + 2 * xx + zl))

    def start_sides(other, later_now, part):
        for away in (2, 1, 3):
            later, copy = side(away, other, part)

            @pl.when(later if later_now else jnp.logical_not(later))
            def _():
                copy.start()

    def to_half(part):
        return kv_copy(OWN, op_there, part, 0, at_seq(row0 + rp))

    def to_up(part):
        return kv_copy(OWN, r, part, 1, at_seq(up + r))

    def op_up(part):
        return kv_copy(op_slot, yp_slot, part, 2, at_seq(up + r))

    def await_part(slot, part):
        kv_copy(OWN, slot, part, 0, at_seq(row0 + rp)).wait_recv()

    for part in (0, 1):
        to_half(part).start()
        to_up(part).start()
    for part in (0, 1):
        start_sides(0, True, part)
    half = ROWS // 2
    a_opp = [
        remote(gb.at[0, pl.ds(i * half, half)], gb.at[2, pl.ds(i * half, half)], a_send.at[i], a_recv.at[i], opposite)
        for i in range(2)
    ]
    a_part = remote(gb.at[0], gb.at[1], a_send.at[2], a_recv.at[2], partner)
    a_fwd = [
        remote(gb.at[2, pl.ds(i * half, half)], gb.at[3, pl.ds(i * half, half)], a_send.at[3 + i], a_recv.at[3 + i], partner)
        for i in range(2)
    ]
    a_part.start()
    for copy in a_opp:
        copy.start()

    mine = order[s]

    def forward(slot, hidden, first=False):
        key = kv[slot, 0]
        value_t = kv[slot, 1].T
        tops = []
        for h in range(RATIO):
            cols = slice(h * ROWS, (h + 1) * ROWS)
            scores = jnp.where(hidden(h), LOWEST, nn(key, qt[:, cols]) * (SCALE * LOG2E))
            st[slot, :, cols] = scores
            tops.append(jnp.max(scores, axis=0, keepdims=True))
        for h in range(RATIO):
            cols = slice(h * ROWS, (h + 1) * ROWS)
            if first:
                top = tops[h]
                probs = jnp.exp2(st[slot, :, cols] - top)
                total[:, cols] = jnp.sum(probs, axis=0, keepdims=True)
                acc[:, cols] = nn(value_t, probs.astype(BF))
            else:
                before = peak[:, cols]
                top = jnp.maximum(before, tops[h])
                fade = jnp.exp2(before - top)
                probs = jnp.exp2(st[slot, :, cols] - top)
                total[:, cols] = total[:, cols] * fade + jnp.sum(probs, axis=0, keepdims=True)
                acc[:, cols] = acc[:, cols] * fade + nn(value_t, probs.astype(BF))
            peak[:, cols] = top

    def forward_on(slot):
        row = jnp.where(slot < r, row0, down)
        gap = (mine - order[row + slot]) * ROWS

        def windowed(h):
            limit = jnp.where(gap > 0, spans[h] - gap, -100000)
            return place[...] >= limit

        forward(slot, windowed)

    def pair_slot(away, other):
        return 2 * ((x + away) % 4) + (zl + other) % 2

    forward(OWN, lambda h: place[...] < 0, first=True)

    for part in (0, 1):
        await_part(op_slot, part)
        op_up(part).start()
        start_sides(1, True, part)
    for part in (0, 1):
        await_part(r, part)
        start_sides(0, False, part)
    forward_on(r)

    loads[4].wait()

    def w_cols(quarter):
        return pl.ds(pl.multiple_of(quarter * 1024, 1024), 1024)

    gsum[...] = nt(gb[0], w[:, w_cols(q0)])
    a_part.wait_recv()
    gsum[...] += nt(gb[1], w[:, w_cols(q1)])

    for part in (0, 1):
        await_part(yp_slot, part)
        start_sides(1, False, part)
    forward_on(rp)

    def forward_step(j, carry):
        away = 3 - 2 * (j % 3) + 3 * ((j % 3) // 2)
        slot = pair_slot(away, j // 3)
        for part in (0, 1):
            await_part(slot, part)
        forward_on(slot)
        return carry

    lax.fori_loop(0, 5, forward_step, 0)
    a_opp[0].wait_recv()
    a_fwd[0].start()
    lax.fori_loop(5, 6, forward_step, 0)
    a_opp[1].wait_recv()
    a_fwd[1].start()

    norm = 1.0 / total[...]
    lse[...] = peak[...] + jnp.log(total[...]) * LOG2E
    for h in range(RATIO):
        cols = slice(h * ROWS, (h + 1) * ROWS)
        mixed = (acc[:, cols] * norm[:, cols]).astype(BF)
        attn[:, h * DIM : (h + 1) * DIM] = mixed.T
        acc[:, cols] = mixed.astype(F32)

    def share(quarter):
        return nn(attn[...], w[:, w_cols(quarter)])

    sh_send[0] = share(f1).astype(BF)
    b_part = [remote(sh_send.at[i], sh_part.at[i], b_send.at[i], b_recv.at[i], partner) for i in range(2)]
    b_part[0].start()

    gsum[...] += nt(gb[2], w[:, w_cols(f0)])
    for copy in a_fwd:
        copy.wait_recv()
    gsum[...] += nt(gb[3], w[:, w_cols(f1)])
    for h in range(RATIO):
        cols = slice(h * ROWS, (h + 1) * ROWS)
        grad = gsum[:, h * DIM : (h + 1) * DIM].astype(BF)
        dos[pl.ds(h * ROWS, ROWS), :] = grad
        grad_t = grad.T
        dot_t[:, cols] = grad_t
        delta[:, cols] = jnp.sum(grad_t.astype(F32) * acc[:, cols], axis=0, keepdims=True)

    def backward(slot):
        key_t = kv[slot, 0].T
        value = kv[slot, 1]
        probs_all = []
        grads_all = []
        for h in range(RATIO):
            cols = slice(h * ROWS, (h + 1) * ROWS)
            probs = jnp.exp2(st[slot, :, cols] - lse[:, cols])
            grad_probs = nn(value, dot_t[:, cols])
            probs_all.append(probs.astype(BF))
            grads_all.append((probs * (grad_probs - delta[:, cols])).astype(BF))
        probs_all = jnp.concatenate(probs_all, axis=1)
        grads_all = jnp.concatenate(grads_all, axis=1)
        grad_key = nn(grads_all, qs[...]) * SCALE
        grad_value = nn(probs_all, dos[...])
        dqt[...] += nn(key_t, grads_all)
        return grad_key, grad_value

    def pair_grads(away, other):
        slot = pair_slot(away, other)
        return remote(
            dsend.at[slot], drecv.at[x, other], d_send.at[slot], d_recv.at[x, other], at_seq(row0 + 2 * ((x + away) % 4) + zl)
        )

    def backward_step(j, carry):
        away, other = 1 + j // 2, 1 - j % 2
        slot = pair_slot(away, other)
        grad_key, grad_value = backward(slot)
        dsend[slot, 0] = grad_key.astype(BF)
        dsend[slot, 1] = grad_value.astype(BF)
        pair_grads(away, other).start()
        return carry

    lax.fori_loop(0, 2, backward_step, 0)
    b_part[0].wait_recv()
    sh_f0[...] = (share(f0) + sh_part[0].astype(F32)).astype(BF)
    b_opp = remote(sh_f0, sh_opp, b_send.at[2], b_recv.at[2], opposite)
    b_opp.start()
    lax.fori_loop(2, 6, backward_step, 0)

    def backward_here(slot, row, other):
        grad_key, grad_value = backward(slot)
        dacc[row, other, 0] = grad_key
        dacc[row, other, 1] = grad_value

    backward_here(rp, 1 - zl, 1)
    backward_here(r, 1, 0)

    def pair_from(index, other):
        return remote(dsend.at[r], drecv.at[index, other], d_send.at[r], d_recv.at[index, other], at_seq(row0 + rp))

    def y_copy(other, part):
        return remote(
            ysend.at[other, part], yrecv.at[other, part], y_send.at[other, part], y_recv.at[other, part], at_seq(down + r)
        )

    def z_copy(part):
        return remote(zsend.at[part], zrecv.at[part], z_send.at[part], z_recv.at[part], at_seq(row0 + rp))

    def add_from(index, row, other):
        pair_from(index, other).wait_recv()
        dacc[row, other] += drecv[index, other].astype(F32)

    def send_up(other):
        @pl.loop(0, x)
        def _(index):
            add_from(x - 1 - index, 1, other)

        for part in (0, 1):
            ysend[other, part] = dacc[1, other, part].astype(BF)
            y_copy(other, part).start()

    has_other = x + 1 - zl > 0
    backward_here(OWN, 0, 0)
    sh_send[1] = share(q1).astype(BF)
    b_part[1].start()
    for h in range(RATIO):
        gq_ref[:, h * DIM : (h + 1) * DIM] = (dqt[:, h * ROWS : (h + 1) * ROWS] * SCALE).astype(BF).T
    whole = share(q0)
    b_part[1].wait_recv()
    gsum_wide = whole + sh_part[1].astype(F32)

    @pl.when(has_other)
    def _():
        send_up(1)

    send_up(0)

    @pl.loop(x + 1, 4)
    def _(index):
        add_from(index, 0, 1)
        add_from(index, 0, 0)

    b_opp.wait_recv()
    out_ref[...] = (gsum_wide + sh_opp[...].astype(F32)).astype(BF)

    for part in (0, 1):

        @pl.when(has_other)
        def _():
            y_copy(1, part).wait_recv()
            zsend[part] = (dacc[0, 1, part] + yrecv[1, part].astype(F32)).astype(BF)

        @pl.when(jnp.logical_not(has_other))
        def _():
            zsend[part] = dacc[0, 1, part].astype(BF)

        z_copy(part).start()

    for part, result in ((0, gk_ref), (1, gv_ref)):
        y_copy(0, part).wait_recv()
        z_copy(part).wait_recv()
        result[...] = (dacc[0, 0, part] + yrecv[0, part].astype(F32) + zrecv[part].astype(F32)).astype(BF)

    for part in (0, 1):
        for copy in (to_half(part), to_up(part), op_up(part), y_copy(0, part), z_copy(part)):
            copy.wait_send()
        for away in (1, 2, 3):
            for other in (0, 1):
                side(away, other, part)[1].wait_send()

        @pl.when(has_other)
        def _():
            y_copy(1, part).wait_send()

    for copy in (a_part, *a_opp, *a_fwd, *b_part, b_opp):
        copy.wait_send()
    for away in (1, 2, 3):
        for other in (0, 1):
            pair_grads(away, other).wait_send()


def finish(*refs):
    ins, outs, sems = refs[:4], refs[4:8], refs[8]
    copies = [pltpu.make_async_copy(a, b, sems.at[i]) for i, (a, b) in enumerate(zip(ins, outs))]
    for copy in copies:
        copy.start()
    for copy in copies:
        copy.wait()


def body(queries, key_vectors, values, out_proj, grad_out, windows, slab_order):
    hbm = pl.BlockSpec(memory_space=pltpu.HBM)
    smem = pl.BlockSpec(memory_space=pltpu.SMEM)
    vmem = pl.BlockSpec(memory_space=pltpu.VMEM)
    wide = RATIO * ROWS
    shapes = ((ROWS, 1024), (ROWS, RATIO * DIM), (ROWS, DIM), (ROWS, DIM))
    results = pl.pallas_call(
        kernel,
        name="layer",
        out_shape=tuple(pltpu.VMEM(shape, BF) for shape in shapes),
        in_specs=[smem, smem, hbm, hbm, hbm, hbm, hbm],
        out_specs=(vmem, vmem, vmem, vmem),
        scratch_shapes=[
            pltpu.VMEM((ROWS, RATIO * DIM), BF),
            pltpu.VMEM((10, 2, ROWS, DIM), BF),
            pltpu.VMEM((RATIO * DIM, 4096), BF),
            pltpu.VMEM((4, ROWS, 1024), BF),
            pltpu.VMEM((DIM, wide), BF),
            pltpu.VMEM((wide, DIM), BF),
            pltpu.VMEM((9, ROWS, wide), F32),
            pltpu.VMEM((1, wide), F32),
            pltpu.VMEM((1, wide), F32),
            pltpu.VMEM((DIM, wide), F32),
            pltpu.VMEM((ROWS, RATIO * DIM), F32),
            pltpu.VMEM((wide, DIM), BF),
            pltpu.VMEM((DIM, wide), BF),
            pltpu.VMEM((1, wide), F32),
            pltpu.VMEM((1, wide), F32),
            pltpu.VMEM((DIM, wide), F32),
            pltpu.VMEM((ROWS, RATIO * DIM), BF),
            pltpu.VMEM((2, ROWS, 1024), BF),
            pltpu.VMEM((ROWS, 1024), BF),
            pltpu.VMEM((2, ROWS, 1024), BF),
            pltpu.VMEM((ROWS, 1024), BF),
            pltpu.VMEM((8, 2, ROWS, DIM), BF),
            pltpu.VMEM((4, 2, 2, ROWS, DIM), BF),
            pltpu.VMEM((2, 2, ROWS, DIM), BF),
            pltpu.VMEM((2, 2, ROWS, DIM), BF),
            pltpu.VMEM((2, ROWS, DIM), BF),
            pltpu.VMEM((2, ROWS, DIM), BF),
            pltpu.VMEM((2, 2, 2, ROWS, DIM), F32),
            pltpu.VMEM((ROWS, ROWS), jnp.int32),
            pltpu.SemaphoreType.DMA((5,)),
            pltpu.SemaphoreType.DMA((9, 2)),
            pltpu.SemaphoreType.DMA((10, 2)),
            pltpu.SemaphoreType.DMA((5,)),
            pltpu.SemaphoreType.DMA((5,)),
            pltpu.SemaphoreType.DMA((3,)),
            pltpu.SemaphoreType.DMA((3,)),
            pltpu.SemaphoreType.DMA((8,)),
            pltpu.SemaphoreType.DMA((4, 2)),
            pltpu.SemaphoreType.DMA((2, 2)),
            pltpu.SemaphoreType.DMA((2, 2)),
            pltpu.SemaphoreType.DMA((2,)),
            pltpu.SemaphoreType.DMA((2,)),
        ],
        compiler_params=pltpu.CompilerParams(collective_id=0, has_side_effects=True, vmem_limit_bytes=56 * 1024 * 1024),
    )(slab_order, windows, queries, key_vectors, values, out_proj, grad_out)
    return pl.pallas_call(
        finish,
        name="finish",
        out_shape=tuple(jax.ShapeDtypeStruct(shape, BF) for shape in shapes),
        in_specs=[vmem] * 4,
        out_specs=(hbm,) * 4,
        scratch_shapes=[pltpu.SemaphoreType.DMA((4,))],
        compiler_params=pltpu.CompilerParams(vmem_limit_bytes=8 * 1024 * 1024),
    )(*results)


def solution(mesh):
    in_specs = (
        P("seq", "head"),
        P("seq", "head"),
        P("seq", "head"),
        P("head", None),
        P("seq", "head"),
        P("head"),
        P(),
    )
    out_specs = (P("seq", "head"), P("seq", "head"), P("seq", "head"), P("seq", "head"))
    return jax.shard_map(body, mesh=mesh, in_specs=in_specs, out_specs=out_specs, check_vma=False)
```

time: 67.8 us -> 52.1 us (0.77)
  the two profiles are of different devices: /device:TPU:56 before, /device:TPU:1 now
where the time goes in v1:
time: 52.1 us; the launch traced here: 52 us
  Pallas kernels  51.4 us (99%)
  between operations  0.64 us (1%)
    pallas_call x1, Pallas kernels, body(): pl.pallas_call(kernel, name='layer', out_shape=tuple((pltpu.VMEM(shape, B...  50.4 us

profile of v1, /device:TPU:1, one launch (start us, length us, event | category | flops | bytes accessed | tf_op | source)
XLA Modules:
  0.0 52.0 jit_solution(18061478124385212368)
XLA Ops:
  0.6 50.4 %layer.1 = (bf16[256,1024]{1,0:T(8,128)(2,1)S(1)}, bf16[256,512]{1,0:T(8,128)(2,1)S(1)}, bf16[256,128]{1,0:T(8,128)(2,1)S(1)}, bf16[256,128]{1,0:T(8,128)(2,1)S(1)}) custom-call(s32[32]{0:T(128)} %order.1, s32[4]{0:T(128)} %spans.1, bf16[256,512]{1,0:T(8,128)(2,1)} %q_hbm.1, bf16[256,128]{1,0:T(8,128)(2,1)} %k_hbm.1, bf16[256,128]{1,0:T(8,128)(2,1)} %v_hbm.1, ...), custom_call_target="tpu_custom_call" | custom-call | tf_op jit(solution)/shard_map/layer/pallas_call | solution.py:394
  51.1 0.9 %finish.1 = (bf16[256,1024]{1,0:T(8,128)(2,1)}, bf16[256,512]{1,0:T(8,128)(2,1)}, bf16[256,128]{1,0:T(8,128)(2,1)}, bf16[256,128]{1,0:T(8,128)(2,1)}) custom-call(bf16[256,1024]{1,0:T(8,128)(2,1)S(1)} %get-tuple-element.8.refs_0_, bf16[256,512]{1,0:T(8,128)(2,1)S(1)} %get-tuple-element.9.refs_1_, bf16[256,128]{1,0:T(8,128)(2,1)S(1)} %get-tuple-element.10.refs_2_, ...), custom_call_target="tpu_custom_call" | custom-call | tf_op jit(solution)/shard_map/finish/pallas_call | solution.py:446

commit v2 on v1

--- a/solution.py
+++ b/solution.py
@@ -26,10 +26,10 @@
 
 
 def kernel(
-    order, spans, q_hbm, k_hbm, v_hbm, w_hbm, g_hbm,
+    order_hbm, spans_hbm, q_hbm, k_hbm, v_hbm, w_hbm, g_hbm,
     out_ref, gq_ref, gk_ref, gv_ref,
     qv, kv, w, gb, qt, qs, st, peak, total, acc, gsum, dos, dot_t, lse, delta, dqt, attn,
-    sh_send, sh_f0, sh_part, sh_opp, dsend, drecv, ysend, yrecv, zsend, zrecv, dacc, place,
+    sh_send, sh_f0, sh_part, sh_opp, dsend, drecv, ysend, yrecv, zsend, zrecv, dacc, place, whole, order, spans,
     lsem, c_send, c_recv, a_send, a_recv, b_send, b_recv, d_send, d_recv, y_send, y_recv, z_send, z_recv,
 ):
     s = lax.axis_index("seq")
@@ -60,6 +60,8 @@
         pltpu.make_async_copy(g_hbm, gb.at[0], lsem.at[2]),
         pltpu.make_async_copy(q_hbm, qv, lsem.at[3]),
         pltpu.make_async_copy(w_hbm, w, lsem.at[4]),
+        pltpu.make_async_copy(order_hbm, order, lsem.at[5]),
+        pltpu.make_async_copy(spans_hbm, spans, lsem.at[6]),
     ]
     for load in loads:
         load.start()
@@ -69,6 +71,74 @@
         pl.semaphore_signal(barrier, inc=1, device_id=at_seq(row0 + (r + 2 * away) % 8), device_id_type=MESH)
     for device in (at_seq(row0 + rp), partner, opposite, at_seq(up + r), at_seq(down + r)):
         pl.semaphore_signal(barrier, inc=1, device_id=device, device_id_type=MESH)
+    edge = jnp.logical_or(x == 0, x == 3)
+
+    @pl.when(edge)
+    def _():
+        corner = jnp.where(x == 3, up + zl, down + 6 + zl)
+        pl.semaphore_signal(barrier, inc=1, device_id=at_seq(corner), device_id_type=MESH)
+
+    pl.semaphore_wait(barrier, jnp.where(edge, 9, 8))
+
+    op_slot = jnp.where(zl == 0, SPARE, r - 1)
+    yp_slot = jnp.where(zl == 0, r + 1, SPARE)
+    op_there = jnp.where(zl == 1, SPARE, r)
+
+    def kv_copy(src, dst, part, send, device):
+        return remote(kv.at[src, part], kv.at[dst, part], c_send.at[send, part], c_recv.at[dst, part], device)
+
+    def side(away, other, part):
+        xx = (x + away) % 4
+        straight = jnp.logical_and(x == 3, away == 1)
+        later = jnp.logical_or(xx > x, straight)
+        row = jnp.where(straight, up, row0)
+        if other:
+            src = jnp.where(later, op_slot, yp_slot)
+        else:
+            src = jnp.where(later, OWN, r)
+        dst = rp if other else r
+        return later, kv_copy(src, dst, part, 3 + 2 * (away - 1) + other, at_seq(row + 2 * xx + zl))
+
+    def start_sides(other, later_now, part):
+        for away in (2, 1, 3):
+            later, copy = side(away, other, part)
+
+            @pl.when(later if later_now else jnp.logical_not(later))
+            def _():
+                copy.start()
+
+    def own_copy(part, dst, send, device):
+        return remote((k_hbm, v_hbm)[part], kv.at[dst, part], c_send.at[send, part], c_recv.at[dst, part], device)
+
+    def to_half(part):
+        return own_copy(part, op_there, 0, at_seq(row0 + rp))
+
+    def to_up(part):
+        return own_copy(part, r, 1, at_seq(up + r))
+
+    def op_up(part):
+        return kv_copy(op_slot, yp_slot, part, 2, at_seq(up + r))
+
+    def await_part(slot, part):
+        kv_copy(OWN, slot, part, 0, at_seq(row0 + rp)).wait_recv()
+
+    for part in (0, 1):
+        to_half(part).start()
+        to_up(part).start()
+    for part in (0, 1):
+        loads[part].wait()
+        start_sides(0, True, part)
+    pieces = 4
+    piece = ROWS // pieces
+    a_opp = [
+        remote(gb.at[0, pl.ds(i * piece, piece)], gb.at[2, pl.ds(i * piece, piece)], a_send.at[i], a_recv.at[i], opposite)
+        for i in range(pieces)
+    ]
+    a_part = remote(gb.at[0], gb.at[1], a_send.at[2 * pieces], a_recv.at[2 * pieces], partner)
+    a_fwd = [
+        remote(gb.at[2, pl.ds(i * piece, piece)], gb.at[3, pl.ds(i * piece, piece)], a_send.at[pieces + i], a_recv.at[pieces + i], partner)
+        for i in range(pieces)
+    ]
     place[...] = lax.broadcasted_iota(jnp.int32, (ROWS, ROWS), 1) - lax.broadcasted_iota(jnp.int32, (ROWS, ROWS), 0)
     dqt[...] = jnp.zeros_like(dqt)
     dacc[zl, 1] = jnp.zeros((2, ROWS, DIM), F32)
@@ -77,66 +147,8 @@
         block = qv[:, h * DIM : (h + 1) * DIM]
         qs[pl.ds(h * ROWS, ROWS), :] = block
         qt[:, h * ROWS : (h + 1) * ROWS] = block.T
-    for i in range(3):
-        loads[i].wait()
-    pl.semaphore_wait(barrier, 8)
-
-    op_slot = jnp.where(zl == 0, SPARE, r - 1)
-    yp_slot = jnp.where(zl == 0, r + 1, SPARE)
-    op_there = jnp.where(zl == 1, SPARE, r)
-
-    def kv_copy(src, dst, part, send, device):
-        return remote(kv.at[src, part], kv.at[dst, part], c_send.at[send, part], c_recv.at[dst, part], device)
-
-    def side(away, other, part):
-        xx = (x + away) % 4
-        later = xx > x
-        if other:
-            src = jnp.where(later, op_slot, yp_slot)
-        else:
-            src = jnp.where(later, OWN, r)
-        dst = rp if other else r
-        return later, kv_copy(src, dst, part, 3 + 2 * (away - 1) + other, at_seq(row0 + 2 * xx + zl))
-
-    def start_sides(other, later_now, part):
-        for away in (2, 1, 3):
-            later, copy = side(away, other, part)
-
-            @pl.when(later if later_now else jnp.logical_not(later))
-            def _():
-                copy.start()
-
-    def to_half(part):
-        return kv_copy(OWN, op_there, part, 0, at_seq(row0 + rp))
-
-    def to_up(part):
-        return kv_copy(OWN, r, part, 1, at_seq(up + r))
-
-    def op_up(part):
-        return kv_copy(op_slot, yp_slot, part, 2, at_seq(up + r))
-
-    def await_part(slot, part):
-        kv_copy(OWN, slot, part, 0, at_seq(row0 + rp)).wait_recv()
-
-    for part in (0, 1):
-        to_half(part).start()
-        to_up(part).start()
-    for part in (0, 1):
-        start_sides(0, True, part)
-    half = ROWS // 2
-    a_opp = [
-        remote(gb.at[0, pl.ds(i * half, half)], gb.at[2, pl.ds(i * half, half)], a_send.at[i], a_recv.at[i], opposite)
-        for i in range(2)
-    ]
-    a_part = remote(gb.at[0], gb.at[1], a_send.at[2], a_recv.at[2], partner)
-    a_fwd = [
-        remote(gb.at[2, pl.ds(i * half, half)], gb.at[3, pl.ds(i * half, half)], a_send.at[3 + i], a_recv.at[3 + i], partner)
-        for i in range(2)
-    ]
-    a_part.start()
-    for copy in a_opp:
-        copy.start()
-
+    loads[5].wait()
+    loads[6].wait()
     mine = order[s]
 
     def forward(slot, hidden, first=False):
@@ -179,14 +191,24 @@
 
     forward(OWN, lambda h: place[...] < 0, first=True)
 
+    loads[2].wait()
+    a_part.start()
+    for copy in a_opp:
+        copy.start()
+
     for part in (0, 1):
         await_part(op_slot, part)
         op_up(part).start()
         start_sides(1, True, part)
-    for part in (0, 1):
-        await_part(r, part)
-        start_sides(0, False, part)
-    forward_on(r)
+    def row_before(slot, other, passing):
+        @pl.when(x > 0 if passing else x == 0)
+        def _():
+            for part in (0, 1):
+                await_part(slot, part)
+                if passing:
+                    start_sides(other, False, part)
+
+    row_before(r, 0, True)
 
     loads[4].wait()
 
@@ -197,10 +219,18 @@
     a_part.wait_recv()
     gsum[...] += nt(gb[1], w[:, w_cols(q1)])
 
-    for part in (0, 1):
-        await_part(yp_slot, part)
-        start_sides(1, False, part)
-    forward_on(rp)
+    def far_columns(group):
+        rows = pl.ds(group * 128, 128)
+        gsum[rows, :] += nt(gb[2, rows, :], w[:, w_cols(f0)])
+        for i in (2 * group, 2 * group + 1):
+            a_fwd[i].wait_recv()
+        gsum[rows, :] += nt(gb[3, rows, :], w[:, w_cols(f1)])
+        for h in range(RATIO):
+            grad = gsum[rows, h * DIM : (h + 1) * DIM].astype(BF)
+            dos[pl.ds(h * ROWS + group * 128, 128), :] = grad
+            dot_t[:, pl.ds(h * ROWS + group * 128, 128)] = grad.T
+
+    row_before(yp_slot, 1, True)
 
     def forward_step(j, carry):
         away = 3 - 2 * (j % 3) + 3 * ((j % 3) // 2)
@@ -210,12 +240,25 @@
         forward_on(slot)
         return carry
 
-    lax.fori_loop(0, 5, forward_step, 0)
-    a_opp[0].wait_recv()
-    a_fwd[0].start()
+    def pass_on(*which):
+        for i in which:
+            a_opp[i].wait_recv()
+            a_fwd[i].start()
+
+    lax.fori_loop(0, 1, forward_step, 0)
+    pass_on(0)
+    lax.fori_loop(1, 2, forward_step, 0)
+    row_before(r, 0, False)
+    forward_on(r)
+    pass_on(1)
+    lax.fori_loop(2, 3, forward_step, 0)
+    row_before(yp_slot, 1, False)
+    forward_on(rp)
+    lax.fori_loop(3, 4, forward_step, 0)
+    pass_on(2)
+    lax.fori_loop(4, 5, forward_step, 0)
+    far_columns(0)
     lax.fori_loop(5, 6, forward_step, 0)
-    a_opp[1].wait_recv()
-    a_fwd[1].start()
 
     norm = 1.0 / total[...]
     lse[...] = peak[...] + jnp.log(total[...]) * LOG2E
@@ -225,24 +268,26 @@
         attn[:, h * DIM : (h + 1) * DIM] = mixed.T
         acc[:, cols] = mixed.astype(F32)
 
-    def share(quarter):
-        return nn(attn[...], w[:, w_cols(quarter)])
-
-    sh_send[0] = share(f1).astype(BF)
-    b_part = [remote(sh_send.at[i], sh_part.at[i], b_send.at[i], b_recv.at[i], partner) for i in range(2)]
-    b_part[0].start()
-
-    gsum[...] += nt(gb[2], w[:, w_cols(f0)])
-    for copy in a_fwd:
-        copy.wait_recv()
-    gsum[...] += nt(gb[3], w[:, w_cols(f1)])
-    for h in range(RATIO):
-        cols = slice(h * ROWS, (h + 1) * ROWS)
-        grad = gsum[:, h * DIM : (h + 1) * DIM].astype(BF)
-        dos[pl.ds(h * ROWS, ROWS), :] = grad
-        grad_t = grad.T
-        dot_t[:, cols] = grad_t
-        delta[:, cols] = jnp.sum(grad_t.astype(F32) * acc[:, cols], axis=0, keepdims=True)
+    def share(quarter, i):
+        return nn(attn[...], w[:, pl.ds(pl.multiple_of(quarter * 1024 + i * 512, 512), 512)])
+
+    def b_part(which, i):
+        return remote(sh_send.at[which, i], sh_part.at[which, i], b_send.at[which, i], b_recv.at[which, i], partner)
+
+    def b_opp(i):
+        return remote(sh_f0.at[i], sh_opp.at[i], b_send.at[2, i], b_recv.at[2, i], opposite)
+
+    def share_out(i):
+        b_part(0, i).wait_recv()
+        sh_f0[i] = (share(f0, i) + sh_part[0, i].astype(F32)).astype(BF)
+        b_opp(i).start()
+
+    pass_on(3)
+    for i in range(2):
+        sh_send[0, i] = share(f1, i).astype(BF)
+        b_part(0, i).start()
+    far_columns(1)
+    delta[...] = jnp.sum(dot_t[...].astype(F32) * acc[...], axis=0, keepdims=True)
 
     def backward(slot):
         key_t = kv[slot, 0].T
@@ -269,7 +314,8 @@
         )
 
     def backward_step(j, carry):
-        away, other = 1 + j // 2, 1 - j % 2
+        turn, other = j % 3, 1 - j // 3
+        away = jnp.where(x == 0, 3 - turn, 2 - turn + 3 * (turn // 2))
         slot = pair_slot(away, other)
         grad_key, grad_value = backward(slot)
         dsend[slot, 0] = grad_key.astype(BF)
@@ -277,11 +323,10 @@
         pair_grads(away, other).start()
         return carry
 
-    lax.fori_loop(0, 2, backward_step, 0)
-    b_part[0].wait_recv()
-    sh_f0[...] = (share(f0) + sh_part[0].astype(F32)).astype(BF)
-    b_opp = remote(sh_f0, sh_opp, b_send.at[2], b_recv.at[2], opposite)
-    b_opp.start()
+    lax.fori_loop(0, 1, backward_step, 0)
+    share_out(0)
+    lax.fori_loop(1, 2, backward_step, 0)
+    share_out(1)
     lax.fori_loop(2, 6, backward_step, 0)
 
     def backward_here(slot, row, other):
@@ -318,14 +363,13 @@
 
     has_other = x + 1 - zl > 0
     backward_here(OWN, 0, 0)
-    sh_send[1] = share(q1).astype(BF)
-    b_part[1].start()
+    for i in range(2):
+        sh_send[1, i] = share(q1, i).astype(BF)
+        b_part(1, i).start()
     for h in range(RATIO):
         gq_ref[:, h * DIM : (h + 1) * DIM] = (dqt[:, h * ROWS : (h + 1) * ROWS] * SCALE).astype(BF).T
-    whole = share(q0)
-    b_part[1].wait_recv()
-    gsum_wide = whole + sh_part[1].astype(F32)
-
+    for i in range(2):
+        whole[i] = share(q0, i)
     @pl.when(has_other)
     def _():
         send_up(1)
@@ -337,9 +381,6 @@
         add_from(index, 0, 1)
         add_from(index, 0, 0)
 
-    b_opp.wait_recv()
-    out_ref[...] = (gsum_wide + sh_opp[...].astype(F32)).astype(BF)
-
     for part in (0, 1):
 
         @pl.when(has_other)
@@ -352,6 +393,11 @@
             zsend[part] = dacc[0, 1, part].astype(BF)
 
         z_copy(part).start()
+
+    for i in range(2):
+        b_part(1, i).wait_recv()
+        b_opp(i).wait_recv()
+        out_ref[:, i * 512 : (i + 1) * 512] = (whole[i] + sh_part[1, i].astype(F32) + sh_opp[i].astype(F32)).astype(BF)
 
     for part, result in ((0, gk_ref), (1, gv_ref)):
         y_copy(0, part).wait_recv()
@@ -369,7 +415,7 @@
         def _():
             y_copy(1, part).wait_send()
 
-    for copy in (a_part, *a_opp, *a_fwd, *b_part, b_opp):
+    for copy in (a_part, *a_opp, *a_fwd, *(b_part(n, i) for n in range(2) for i in range(2)), b_opp(0), b_opp(1)):
         copy.wait_send()
     for away in (1, 2, 3):
         for other in (0, 1):
@@ -387,7 +433,6 @@
 
 def body(queries, key_vectors, values, out_proj, grad_out, windows, slab_order):
     hbm = pl.BlockSpec(memory_space=pltpu.HBM)
-    smem = pl.BlockSpec(memory_space=pltpu.SMEM)
     vmem = pl.BlockSpec(memory_space=pltpu.VMEM)
     wide = RATIO * ROWS
     shapes = ((ROWS, 1024), (ROWS, RATIO * DIM), (ROWS, DIM), (ROWS, DIM))
@@ -395,7 +440,7 @@
         kernel,
         name="layer",
         out_shape=tuple(pltpu.VMEM(shape, BF) for shape in shapes),
-        in_specs=[smem, smem, hbm, hbm, hbm, hbm, hbm],
+        in_specs=[hbm] * 7,
         out_specs=(vmem, vmem, vmem, vmem),
         scratch_shapes=[
             pltpu.VMEM((ROWS, RATIO * DIM), BF),
@@ -415,10 +460,10 @@
             pltpu.VMEM((1, wide), F32),
             pltpu.VMEM((DIM, wide), F32),
             pltpu.VMEM((ROWS, RATIO * DIM), BF),
-            pltpu.VMEM((2, ROWS, 1024), BF),
-            pltpu.VMEM((ROWS, 1024), BF),
-            pltpu.VMEM((2, ROWS, 1024), BF),
-            pltpu.VMEM((ROWS, 1024), BF),
+            pltpu.VMEM((2, 2, ROWS, 512), BF),
+            pltpu.VMEM((2, ROWS, 512), BF),
+            pltpu.VMEM((2, 2, ROWS, 512), BF),
+            pltpu.VMEM((2, ROWS, 512), BF),
             pltpu.VMEM((8, 2, ROWS, DIM), BF),
             pltpu.VMEM((4, 2, 2, ROWS, DIM), BF),
             pltpu.VMEM((2, 2, ROWS, DIM), BF),
@@ -427,13 +472,16 @@
             pltpu.VMEM((2, ROWS, DIM), BF),
             pltpu.VMEM((2, 2, 2, ROWS, DIM), F32),
             pltpu.VMEM((ROWS, ROWS), jnp.int32),
-            pltpu.SemaphoreType.DMA((5,)),
+            pltpu.VMEM((2, ROWS, 512), F32),
+            pltpu.SMEM((32,), jnp.int32),
+            pltpu.SMEM((RATIO,), jnp.int32),
+            pltpu.SemaphoreType.DMA((7,)),
             pltpu.SemaphoreType.DMA((9, 2)),
             pltpu.SemaphoreType.DMA((10, 2)),
-            pltpu.SemaphoreType.DMA((5,)),
-            pltpu.SemaphoreType.DMA((5,)),
-            pltpu.SemaphoreType.DMA((3,)),
-            pltpu.SemaphoreType.DMA((3,)),
+            pltpu.SemaphoreType.DMA((9,)),
+            pltpu.SemaphoreType.DMA((9,)),
+            pltpu.SemaphoreType.DMA((3, 2)),
+            pltpu.SemaphoreType.DMA((3, 2)),
             pltpu.SemaphoreType.DMA((8,)),
             pltpu.SemaphoreType.DMA((4, 2)),
             pltpu.SemaphoreType.DMA((2, 2)),

time: 52.1 us -> 47.9 us (0.919)
  the two profiles are of different devices: /device:TPU:1 before, /device:TPU:2 now
where the time goes in v2:
time: 47.9 us; the launch traced here: 47.8 us
  Pallas kernels  47.2 us (99%)
  between operations  0.64 us (1%)
    pallas_call x1, Pallas kernels, body(): pl.pallas_call(kernel, name='layer', out_shape=tuple((pltpu.VMEM(shape, B...  46.2 us

profile of v2, /device:TPU:2, one launch (start us, length us, event | category | flops | bytes accessed | tf_op | source)
XLA Modules:
  0.0 47.8 jit_solution(13209460913846166218)
XLA Ops:
  0.6 46.2 %layer.1 = (bf16[256,1024]{1,0:T(8,128)(2,1)S(1)}, bf16[256,512]{1,0:T(8,128)(2,1)S(1)}, bf16[256,128]{1,0:T(8,128)(2,1)S(1)}, bf16[256,128]{1,0:T(8,128)(2,1)S(1)}) custom-call(s32[32]{0:T(128)} %order_hbm.1, s32[4]{0:T(128)} %spans_hbm.1, bf16[256,512]{1,0:T(8,128)(2,1)} %q_hbm.1, bf16[256,128]{1,0:T(8,128)(2,1)} %k_hbm.1, bf16[256,128]{1,0:T(8,128)(2,1)} %v_hbm.1, ...), custom_call_target="tpu_custom_call" | custom-call | tf_op jit(solution)/shard_map/layer/pallas_call | solution.py:439
  46.8 0.9 %finish.1 = (bf16[256,1024]{1,0:T(8,128)(2,1)}, bf16[256,512]{1,0:T(8,128)(2,1)}, bf16[256,128]{1,0:T(8,128)(2,1)}, bf16[256,128]{1,0:T(8,128)(2,1)}) custom-call(bf16[256,1024]{1,0:T(8,128)(2,1)S(1)} %get-tuple-element.8.refs_0_, bf16[256,512]{1,0:T(8,128)(2,1)S(1)} %get-tuple-element.9.refs_1_, bf16[256,128]{1,0:T(8,128)(2,1)S(1)} %get-tuple-element.10.refs_2_, ...), custom_call_target="tpu_custom_call" | custom-call | tf_op jit(solution)/shard_map/finish/pallas_call | solution.py:494

commit v3 on v2

--- a/solution.py
+++ b/solution.py
@@ -232,33 +232,52 @@
 
     row_before(yp_slot, 1, True)
 
-    def forward_step(j, carry):
-        away = 3 - 2 * (j % 3) + 3 * ((j % 3) // 2)
-        slot = pair_slot(away, j // 3)
-        for part in (0, 1):
-            await_part(slot, part)
-        forward_on(slot)
-        return carry
-
     def pass_on(*which):
         for i in which:
             a_opp[i].wait_recv()
             a_fwd[i].start()
 
-    lax.fori_loop(0, 1, forward_step, 0)
+    orders = (
+        ((3, 0), (1, 0), 0, (2, 0), 1, (3, 1), (1, 1), (2, 1)),
+        (0, 1, (3, 0), (3, 1), (1, 0), (2, 0), (1, 1), (2, 1)),
+        (0, 1, (3, 0), (2, 0), (3, 1), (2, 1), (1, 0), (1, 1)),
+        (0, 1, (3, 0), (2, 0), (1, 0), (3, 1), (2, 1), (1, 1)),
+    )
+
+    def by_x(values):
+        return jnp.where(x == 0, values[0], jnp.where(x == 1, values[1], jnp.where(x == 2, values[2], values[3])))
+
+    def slot_of(what):
+        if what == 0:
+            return r
+        return rp if what == 1 else pair_slot(*what)
+
+    def forward_step(i):
+        picks = [order_x[i] for order_x in orders]
+        slot = by_x([slot_of(what) for what in picks])
+        paired = by_x([int(isinstance(what, tuple)) for what in picks])
+
+        @pl.when(paired == 1)
+        def _():
+            for part in (0, 1):
+                await_part(slot, part)
+
+        if i == 2:
+            row_before(r, 0, False)
+        if i == 4:
+            row_before(yp_slot, 1, False)
+        forward_on(slot)
+
+    for i in range(3):
+        forward_step(i)
     pass_on(0)
-    lax.fori_loop(1, 2, forward_step, 0)
-    row_before(r, 0, False)
-    forward_on(r)
+    forward_step(3)
     pass_on(1)
-    lax.fori_loop(2, 3, forward_step, 0)
-    row_before(yp_slot, 1, False)
-    forward_on(rp)
-    lax.fori_loop(3, 4, forward_step, 0)
+    forward_step(4)
+    forward_step(5)
     pass_on(2)
-    lax.fori_loop(4, 5, forward_step, 0)
-    far_columns(0)
-    lax.fori_loop(5, 6, forward_step, 0)
+    forward_step(6)
+    forward_step(7)
 
     norm = 1.0 / total[...]
     lse[...] = peak[...] + jnp.log(total[...]) * LOG2E
@@ -286,6 +305,7 @@
     for i in range(2):
         sh_send[0, i] = share(f1, i).astype(BF)
         b_part(0, i).start()
+    far_columns(0)
     far_columns(1)
     delta[...] = jnp.sum(dot_t[...].astype(F32) * acc[...], axis=0, keepdims=True)
 
@@ -307,27 +327,40 @@
         dqt[...] += nn(key_t, grads_all)
         return grad_key, grad_value
 
-    def pair_grads(away, other):
+    def pair_grads(away, other, part):
         slot = pair_slot(away, other)
         return remote(
-            dsend.at[slot], drecv.at[x, other], d_send.at[slot], d_recv.at[x, other], at_seq(row0 + 2 * ((x + away) % 4) + zl)
+            dsend.at[slot, part],
+            drecv.at[x, other, part],
+            d_send.at[slot, part],
+            d_recv.at[x, other, part],
+            at_seq(row0 + 2 * ((x + away) % 4) + zl),
         )
 
+    def turn_away(turn):
+        return jnp.where(x == 0, 3 - turn, 2 - turn + 3 * (turn // 2))
+
     def backward_step(j, carry):
-        turn, other = j % 3, 1 - j // 3
-        away = jnp.where(x == 0, 3 - turn, 2 - turn + 3 * (turn // 2))
+        other = 1 - j // 3
+        away = turn_away(j % 3)
         slot = pair_slot(away, other)
         grad_key, grad_value = backward(slot)
         dsend[slot, 0] = grad_key.astype(BF)
+        pair_grads(away, other, 0).start()
         dsend[slot, 1] = grad_value.astype(BF)
-        pair_grads(away, other).start()
+
+        @pl.when(other == 1)
+        def _():
+            pair_grads(away, other, 1).start()
+
         return carry
 
-    lax.fori_loop(0, 1, backward_step, 0)
     share_out(0)
-    lax.fori_loop(1, 2, backward_step, 0)
+    lax.fori_loop(0, 2, backward_step, 0)
     share_out(1)
     lax.fori_loop(2, 6, backward_step, 0)
+    for turn in range(3):
+        pair_grads(turn_away(turn), 0, 1).start()
 
     def backward_here(slot, row, other):
         grad_key, grad_value = backward(slot)
@@ -337,8 +370,10 @@
     backward_here(rp, 1 - zl, 1)
     backward_here(r, 1, 0)
 
-    def pair_from(index, other):
-        return remote(dsend.at[r], drecv.at[index, other], d_send.at[r], d_recv.at[index, other], at_seq(row0 + rp))
+    def pair_from(index, other, part):
+        return remote(
+            dsend.at[r, part], drecv.at[index, other, part], d_send.at[r, part], d_recv.at[index, other, part], at_seq(row0 + rp)
+        )
 
     def y_copy(other, part):
         return remote(
@@ -348,18 +383,22 @@
     def z_copy(part):
         return remote(zsend.at[part], zrecv.at[part], z_send.at[part], z_recv.at[part], at_seq(row0 + rp))
 
-    def add_from(index, row, other):
-        pair_from(index, other).wait_recv()
-        dacc[row, other] += drecv[index, other].astype(F32)
-
-    def send_up(other):
+    def add_from(index, row, other, part):
+        pair_from(index, other, part).wait_recv()
+        dacc[row, other, part] += drecv[index, other, part].astype(F32)
+
+    def send_up(other, part):
         @pl.loop(0, x)
         def _(index):
-            add_from(x - 1 - index, 1, other)
-
-        for part in (0, 1):
-            ysend[other, part] = dacc[1, other, part].astype(BF)
-            y_copy(other, part).start()
+            add_from(x - 1 - index, 1, other, part)
+
+        ysend[other, part] = dacc[1, other, part].astype(BF)
+        y_copy(other, part).start()
+
+    def add_later(other, part):
+        @pl.loop(x + 1, 4)
+        def _(index):
+            add_from(index, 0, other, part)
 
     has_other = x + 1 - zl > 0
     backward_here(OWN, 0, 0)
@@ -372,14 +411,13 @@
         whole[i] = share(q0, i)
     @pl.when(has_other)
     def _():
-        send_up(1)
-
-    send_up(0)
-
-    @pl.loop(x + 1, 4)
-    def _(index):
-        add_from(index, 0, 1)
-        add_from(index, 0, 0)
+        for part in (0, 1):
+            send_up(1, part)
+
+    for part in (0, 1):
+        add_later(1, part)
+    send_up(0, 0)
+    add_later(0, 0)
 
     for part in (0, 1):
 
@@ -394,32 +432,39 @@
 
         z_copy(part).start()
 
+    send_up(0, 1)
+    add_later(0, 1)
+
     for i in range(2):
         b_part(1, i).wait_recv()
         b_opp(i).wait_recv()
         out_ref[:, i * 512 : (i + 1) * 512] = (whole[i] + sh_part[1, i].astype(F32) + sh_opp[i].astype(F32)).astype(BF)
 
+    for part in (0, 1):
+        for copy in (to_half(part), to_up(part), op_up(part)):
+            copy.wait_send()
+        for away in (1, 2, 3):
+            for other in (0, 1):
+                side(away, other, part)[1].wait_send()
+
+        @pl.when(has_other)
+        def _():
+            y_copy(1, part).wait_send()
+
+    for copy in (a_part, *a_opp, *a_fwd, *(b_part(n, i) for n in range(2) for i in range(2)), b_opp(0), b_opp(1)):
+        copy.wait_send()
+    for away in (1, 2, 3):
+        for other in (0, 1):
+            for part in (0, 1):
+                pair_grads(away, other, part).wait_send()
+    for part in (0, 1):
+        y_copy(0, part).wait_send()
+        z_copy(part).wait_send()
+
     for part, result in ((0, gk_ref), (1, gv_ref)):
         y_copy(0, part).wait_recv()
         z_copy(part).wait_recv()
         result[...] = (dacc[0, 0, part] + yrecv[0, part].astype(F32) + zrecv[part].astype(F32)).astype(BF)
-
-    for part in (0, 1):
-        for copy in (to_half(part), to_up(part), op_up(part), y_copy(0, part), z_copy(part)):
-            copy.wait_send()
-        for away in (1, 2, 3):
-            for other in (0, 1):
-                side(away, other, part)[1].wait_send()
-
-        @pl.when(has_other)
-        def _():
-            y_copy(1, part).wait_send()
-
-    for copy in (a_part, *a_opp, *a_fwd, *(b_part(n, i) for n in range(2) for i in range(2)), b_opp(0), b_opp(1)):
-        copy.wait_send()
-    for away in (1, 2, 3):
-        for other in (0, 1):
-            pair_grads(away, other).wait_send()
 
 
 def finish(*refs):
@@ -482,8 +527,8 @@
             pltpu.SemaphoreType.DMA((9,)),
             pltpu.SemaphoreType.DMA((3, 2)),
             pltpu.SemaphoreType.DMA((3, 2)),
-            pltpu.SemaphoreType.DMA((8,)),
-            pltpu.SemaphoreType.DMA((4, 2)),
+            pltpu.SemaphoreType.DMA((8, 2)),
+            pltpu.SemaphoreType.DMA((4, 2, 2)),
             pltpu.SemaphoreType.DMA((2, 2)),
             pltpu.SemaphoreType.DMA((2, 2)),
             pltpu.SemaphoreType.DMA((2,)),

time: 47.9 us -> 45.5 us (0.950)
  Pallas kernels: 47.2 us -> 44.5 us
    pallas_call x1, Pallas kernels: 46.2 us -> 43.6 us  [body(): pl.pallas_call(kernel, name='layer', out_shape=tuple((pltpu.VMEM(shape, B...]
where the time goes in v3:
time: 45.5 us; the launch traced here: 45.1 us
  Pallas kernels  44.5 us (98%)
  between operations  0.64 us (1%)
    pallas_call x1, Pallas kernels, body(): pl.pallas_call(kernel, name='layer', out_shape=tuple((pltpu.VMEM(shape, B...  43.6 us
    pallas_call x1, Pallas kernels, body(): pl.pallas_call(finish, name='finish', out_shape=tuple((jax.ShapeDtypeStru...  0.95 us

profile of v3, /device:TPU:2, one launch (start us, length us, event | category | flops | bytes accessed | tf_op | source)
XLA Modules:
  0.0 45.1 jit_solution(14840979400717858065)
XLA Ops:
  0.6 43.6 %layer.1 = (bf16[256,1024]{1,0:T(8,128)(2,1)S(1)}, bf16[256,512]{1,0:T(8,128)(2,1)S(1)}, bf16[256,128]{1,0:T(8,128)(2,1)S(1)}, bf16[256,128]{1,0:T(8,128)(2,1)S(1)}) custom-call(s32[32]{0:T(128)} %order_hbm.1, s32[4]{0:T(128)} %spans_hbm.1, bf16[256,512]{1,0:T(8,128)(2,1)} %q_hbm.1, bf16[256,128]{1,0:T(8,128)(2,1)} %k_hbm.1, bf16[256,128]{1,0:T(8,128)(2,1)} %v_hbm.1, ...), custom_call_target="tpu_custom_call" | custom-call | tf_op jit(solution)/shard_map/layer/pallas_call | solution.py:484
  44.2 0.9 %finish.1 = (bf16[256,1024]{1,0:T(8,128)(2,1)}, bf16[256,512]{1,0:T(8,128)(2,1)}, bf16[256,128]{1,0:T(8,128)(2,1)}, bf16[256,128]{1,0:T(8,128)(2,1)}) custom-call(bf16[256,1024]{1,0:T(8,128)(2,1)S(1)} %get-tuple-element.8.refs_0_, bf16[256,512]{1,0:T(8,128)(2,1)S(1)} %get-tuple-element.9.refs_1_, bf16[256,128]{1,0:T(8,128)(2,1)S(1)} %get-tuple-element.10.refs_2_, ...), custom_call_target="tpu_custom_call" | custom-call | tf_op jit(solution)/shard_map/finish/pallas_call | solution.py:539

commit v4 on v3

--- a/solution.py
+++ b/solution.py
@@ -85,7 +85,7 @@
     op_there = jnp.where(zl == 1, SPARE, r)
 
     def kv_copy(src, dst, part, send, device):
-        return remote(kv.at[src, part], kv.at[dst, part], c_send.at[send, part], c_recv.at[dst, part], device)
+        return remote(kv.at[src, part], kv.at[dst, part], c_send, c_recv.at[dst, part], device)
 
     def side(away, other, part):
         xx = (x + away) % 4
@@ -108,7 +108,7 @@
                 copy.start()
 
     def own_copy(part, dst, send, device):
-        return remote((k_hbm, v_hbm)[part], kv.at[dst, part], c_send.at[send, part], c_recv.at[dst, part], device)
+        return remote((k_hbm, v_hbm)[part], kv.at[dst, part], c_send, c_recv.at[dst, part], device)
 
     def to_half(part):
         return own_copy(part, op_there, 0, at_seq(row0 + rp))
@@ -131,12 +131,12 @@
     pieces = 4
     piece = ROWS // pieces
     a_opp = [
-        remote(gb.at[0, pl.ds(i * piece, piece)], gb.at[2, pl.ds(i * piece, piece)], a_send.at[i], a_recv.at[i], opposite)
+        remote(gb.at[0, pl.ds(i * piece, piece)], gb.at[2, pl.ds(i * piece, piece)], a_send, a_recv.at[i], opposite)
         for i in range(pieces)
     ]
-    a_part = remote(gb.at[0], gb.at[1], a_send.at[2 * pieces], a_recv.at[2 * pieces], partner)
+    a_part = remote(gb.at[0], gb.at[1], a_send, a_recv.at[2 * pieces], partner)
     a_fwd = [
-        remote(gb.at[2, pl.ds(i * piece, piece)], gb.at[3, pl.ds(i * piece, piece)], a_send.at[pieces + i], a_recv.at[pieces + i], partner)
+        remote(gb.at[2, pl.ds(i * piece, piece)], gb.at[3, pl.ds(i * piece, piece)], a_send, a_recv.at[pieces + i], partner)
         for i in range(pieces)
     ]
     place[...] = lax.broadcasted_iota(jnp.int32, (ROWS, ROWS), 1) - lax.broadcasted_iota(jnp.int32, (ROWS, ROWS), 0)
@@ -291,10 +291,10 @@
         return nn(attn[...], w[:, pl.ds(pl.multiple_of(quarter * 1024 + i * 512, 512), 512)])
 
     def b_part(which, i):
-        return remote(sh_send.at[which, i], sh_part.at[which, i], b_send.at[which, i], b_recv.at[which, i], partner)
+        return remote(sh_send.at[which, i], sh_part.at[which, i], b_send, b_recv.at[which, i], partner)
 
     def b_opp(i):
-        return remote(sh_f0.at[i], sh_opp.at[i], b_send.at[2, i], b_recv.at[2, i], opposite)
+        return remote(sh_f0.at[i], sh_opp.at[i], b_send, b_recv.at[2, i], opposite)
 
     def share_out(i):
         b_part(0, i).wait_recv()
@@ -332,7 +332,7 @@
         return remote(
             dsend.at[slot, part],
             drecv.at[x, other, part],
-            d_send.at[slot, part],
+            d_send,
             d_recv.at[x, other, part],
             at_seq(row0 + 2 * ((x + away) % 4) + zl),
         )
@@ -372,16 +372,16 @@
 
     def pair_from(index, other, part):
         return remote(
-            dsend.at[r, part], drecv.at[index, other, part], d_send.at[r, part], d_recv.at[index, other, part], at_seq(row0 + rp)
+            dsend.at[r, part], drecv.at[index, other, part], d_send, d_recv.at[index, other, part], at_seq(row0 + rp)
         )
 
     def y_copy(other, part):
         return remote(
-            ysend.at[other, part], yrecv.at[other, part], y_send.at[other, part], y_recv.at[other, part], at_seq(down + r)
+            ysend.at[other, part], yrecv.at[other, part], y_send, y_recv.at[other, part], at_seq(down + r)
         )
 
     def z_copy(part):
-        return remote(zsend.at[part], zrecv.at[part], z_send.at[part], z_recv.at[part], at_seq(row0 + rp))
+        return remote(zsend.at[part], zrecv.at[part], z_send, z_recv.at[part], at_seq(row0 + rp))
 
     def add_from(index, row, other, part):
         pair_from(index, other, part).wait_recv()
@@ -440,26 +440,22 @@
         b_opp(i).wait_recv()
         out_ref[:, i * 512 : (i + 1) * 512] = (whole[i] + sh_part[1, i].astype(F32) + sh_opp[i].astype(F32)).astype(BF)
 
-    for part in (0, 1):
-        for copy in (to_half(part), to_up(part), op_up(part)):
-            copy.wait_send()
-        for away in (1, 2, 3):
-            for other in (0, 1):
-                side(away, other, part)[1].wait_send()
-
-        @pl.when(has_other)
-        def _():
-            y_copy(1, part).wait_send()
-
-    for copy in (a_part, *a_opp, *a_fwd, *(b_part(n, i) for n in range(2) for i in range(2)), b_opp(0), b_opp(1)):
-        copy.wait_send()
-    for away in (1, 2, 3):
-        for other in (0, 1):
-            for part in (0, 1):
-                pair_grads(away, other, part).wait_send()
-    for part in (0, 1):
-        y_copy(0, part).wait_send()
-        z_copy(part).wait_send()
+    def all_left(ref, send, recv):
+        remote(ref, ref, send, recv, at_seq(row0 + rp)).wait_send()
+
+    all_left(kv.at[pl.ds(0, 9)], c_send, c_recv.at[0, 0])
+    all_left(gb.at[pl.ds(0, 3)], a_send, a_recv.at[0])
+    all_left(gb.at[pl.ds(0, 3)], b_send, b_recv.at[0, 0])
+    all_left(dsend.at[pl.ds(0, 6)], d_send, d_recv.at[0, 0, 0])
+    all_left(zsend, z_send, z_recv.at[0])
+
+    @pl.when(has_other)
+    def _():
+        all_left(ysend, y_send, y_recv.at[0, 0])
+
+    @pl.when(jnp.logical_not(has_other))
+    def _():
+        all_left(ysend.at[0], y_send, y_recv.at[0, 0])
 
     for part, result in ((0, gk_ref), (1, gv_ref)):
         y_copy(0, part).wait_recv()
@@ -521,17 +517,17 @@
             pltpu.SMEM((32,), jnp.int32),
             pltpu.SMEM((RATIO,), jnp.int32),
             pltpu.SemaphoreType.DMA((7,)),
-            pltpu.SemaphoreType.DMA((9, 2)),
+            pltpu.SemaphoreType.DMA,
             pltpu.SemaphoreType.DMA((10, 2)),
+            pltpu.SemaphoreType.DMA,
             pltpu.SemaphoreType.DMA((9,)),
-            pltpu.SemaphoreType.DMA((9,)),
+            pltpu.SemaphoreType.DMA,
             pltpu.SemaphoreType.DMA((3, 2)),
-            pltpu.SemaphoreType.DMA((3, 2)),
-            pltpu.SemaphoreType.DMA((8, 2)),
+            pltpu.SemaphoreType.DMA,
             pltpu.SemaphoreType.DMA((4, 2, 2)),
+            pltpu.SemaphoreType.DMA,
             pltpu.SemaphoreType.DMA((2, 2)),
-            pltpu.SemaphoreType.DMA((2, 2)),
-            pltpu.SemaphoreType.DMA((2,)),
+            pltpu.SemaphoreType.DMA,
             pltpu.SemaphoreType.DMA((2,)),
         ],
         compiler_params=pltpu.CompilerParams(collective_id=0, has_side_effects=True, vmem_limit_bytes=56 * 1024 * 1024),

time: 45.5 us -> 45 us (0.989)
  no operation moved by 1% of the time
where the time goes in v4:
time: 45 us; the launch traced here: 44.7 us
  Pallas kernels  44.1 us (98%)
  between operations  0.64 us (1%)
    pallas_call x1, Pallas kernels, body(): pl.pallas_call(kernel, name='layer', out_shape=tuple((pltpu.VMEM(shape, B...  43.1 us
    pallas_call x1, Pallas kernels, body(): pl.pallas_call(finish, name='finish', out_shape=tuple((jax.ShapeDtypeStru...  0.95 us

profile of v4, /device:TPU:2, one launch (start us, length us, event | category | flops | bytes accessed | tf_op | source)
XLA Modules:
  0.0 44.7 jit_solution(11111559611989092696)
XLA Ops:
  0.6 43.1 %layer.1 = (bf16[256,1024]{1,0:T(8,128)(2,1)S(1)}, bf16[256,512]{1,0:T(8,128)(2,1)S(1)}, bf16[256,128]{1,0:T(8,128)(2,1)S(1)}, bf16[256,128]{1,0:T(8,128)(2,1)S(1)}) custom-call(s32[32]{0:T(128)} %order_hbm.1, s32[4]{0:T(128)} %spans_hbm.1, bf16[256,512]{1,0:T(8,128)(2,1)} %q_hbm.1, bf16[256,128]{1,0:T(8,128)(2,1)} %k_hbm.1, bf16[256,128]{1,0:T(8,128)(2,1)} %v_hbm.1, ...), custom_call_target="tpu_custom_call" | custom-call | tf_op jit(solution)/shard_map/layer/pallas_call | solution.py:480
  43.7 0.9 %finish.1 = (bf16[256,1024]{1,0:T(8,128)(2,1)}, bf16[256,512]{1,0:T(8,128)(2,1)}, bf16[256,128]{1,0:T(8,128)(2,1)}, bf16[256,128]{1,0:T(8,128)(2,1)}) custom-call(bf16[256,1024]{1,0:T(8,128)(2,1)S(1)} %get-tuple-element.8.refs_0_, bf16[256,512]{1,0:T(8,128)(2,1)S(1)} %get-tuple-element.9.refs_1_, bf16[256,128]{1,0:T(8,128)(2,1)S(1)} %get-tuple-element.10.refs_2_, ...), custom_call_target="tpu_custom_call" | custom-call | tf_op jit(solution)/shard_map/finish/pallas_call | solution.py:535

commit v5 on v4

--- a/solution.py
+++ b/solution.py
@@ -241,7 +241,7 @@
         ((3, 0), (1, 0), 0, (2, 0), 1, (3, 1), (1, 1), (2, 1)),
         (0, 1, (3, 0), (3, 1), (1, 0), (2, 0), (1, 1), (2, 1)),
         (0, 1, (3, 0), (2, 0), (3, 1), (2, 1), (1, 0), (1, 1)),
-        (0, 1, (3, 0), (2, 0), (1, 0), (3, 1), (2, 1), (1, 1)),
+        (0, 1, (3, 0), (3, 1), (2, 0), (1, 0), (2, 1), (1, 1)),
     )
 
     def by_x(values):

time: 45 us -> 45 us (level)
  no operation moved by 1% of the time
where the time goes in v5:
time: 45 us; the launch traced here: 44.7 us
  Pallas kernels  44.1 us (98%)
  between operations  0.64 us (1%)
    pallas_call x1, Pallas kernels, body(): pl.pallas_call(kernel, name='layer', out_shape=tuple((pltpu.VMEM(shape, B...  43.1 us
    pallas_call x1, Pallas kernels, body(): pl.pallas_call(finish, name='finish', out_shape=tuple((jax.ShapeDtypeStru...  0.95 us

profile of v5, /device:TPU:2, one launch (start us, length us, event | category | flops | bytes accessed | tf_op | source)
XLA Modules:
  0.0 44.7 jit_solution(2401956413853640669)
XLA Ops:
  0.6 43.1 %layer.1 = (bf16[256,1024]{1,0:T(8,128)(2,1)S(1)}, bf16[256,512]{1,0:T(8,128)(2,1)S(1)}, bf16[256,128]{1,0:T(8,128)(2,1)S(1)}, bf16[256,128]{1,0:T(8,128)(2,1)S(1)}) custom-call(s32[32]{0:T(128)} %order_hbm.1, s32[4]{0:T(128)} %spans_hbm.1, bf16[256,512]{1,0:T(8,128)(2,1)} %q_hbm.1, bf16[256,128]{1,0:T(8,128)(2,1)} %k_hbm.1, bf16[256,128]{1,0:T(8,128)(2,1)} %v_hbm.1, ...), custom_call_target="tpu_custom_call" | custom-call | tf_op jit(solution)/shard_map/layer/pallas_call | solution.py:480
  43.7 0.9 %finish.1 = (bf16[256,1024]{1,0:T(8,128)(2,1)}, bf16[256,512]{1,0:T(8,128)(2,1)}, bf16[256,128]{1,0:T(8,128)(2,1)}, bf16[256,128]{1,0:T(8,128)(2,1)}) custom-call(bf16[256,1024]{1,0:T(8,128)(2,1)S(1)} %get-tuple-element.8.refs_0_, bf16[256,512]{1,0:T(8,128)(2,1)S(1)} %get-tuple-element.9.refs_1_, bf16[256,128]{1,0:T(8,128)(2,1)S(1)} %get-tuple-element.10.refs_2_, ...), custom_call_target="tpu_custom_call" | custom-call | tf_op jit(solution)/shard_map/finish/pallas_call | solution.py:535

commit v6 on v4

--- a/solution.py
+++ b/solution.py
@@ -129,14 +129,14 @@
         loads[part].wait()
         start_sides(0, True, part)
     pieces = 4
-    piece = ROWS // pieces
+    cuts = (0, 80, 160, 224, ROWS)
     a_opp = [
-        remote(gb.at[0, pl.ds(i * piece, piece)], gb.at[2, pl.ds(i * piece, piece)], a_send, a_recv.at[i], opposite)
+        remote(gb.at[0, pl.ds(cuts[i], cuts[i + 1] - cuts[i])], gb.at[2, pl.ds(cuts[i], cuts[i + 1] - cuts[i])], a_send, a_recv.at[i], opposite)
         for i in range(pieces)
     ]
     a_part = remote(gb.at[0], gb.at[1], a_send, a_recv.at[2 * pieces], partner)
     a_fwd = [
-        remote(gb.at[2, pl.ds(i * piece, piece)], gb.at[3, pl.ds(i * piece, piece)], a_send, a_recv.at[pieces + i], partner)
+        remote(gb.at[2, pl.ds(cuts[i], cuts[i + 1] - cuts[i])], gb.at[3, pl.ds(cuts[i], cuts[i + 1] - cuts[i])], a_send, a_recv.at[pieces + i], partner)
         for i in range(pieces)
     ]
     place[...] = lax.broadcasted_iota(jnp.int32, (ROWS, ROWS), 1) - lax.broadcasted_iota(jnp.int32, (ROWS, ROWS), 0)

time: 45 us -> 45.7 us (1.016)
  Pallas kernels: 44.1 us -> 44.7 us
    pallas_call x1, Pallas kernels: 43.1 us -> 43.7 us  [body(): pl.pallas_call(kernel, name='layer', out_shape=tuple((pltpu.VMEM(shape, B...]
where the time goes in v6:
time: 45.7 us; the launch traced here: 45.3 us
  Pallas kernels  44.7 us (98%)
  between operations  0.64 us (1%)
    pallas_call x1, Pallas kernels, body(): pl.pallas_call(kernel, name='layer', out_shape=tuple((pltpu.VMEM(shape, B...  43.7 us
    pallas_call x1, Pallas kernels, body(): pl.pallas_call(finish, name='finish', out_shape=tuple((jax.ShapeDtypeStru...  0.95 us

profile of v6, /device:TPU:2, one launch (start us, length us, event | category | flops | bytes accessed | tf_op | source)
XLA Modules:
  0.0 45.3 jit_solution(7608806051286034836)
XLA Ops:
  0.6 43.7 %layer.1 = (bf16[256,1024]{1,0:T(8,128)(2,1)S(1)}, bf16[256,512]{1,0:T(8,128)(2,1)S(1)}, bf16[256,128]{1,0:T(8,128)(2,1)S(1)}, bf16[256,128]{1,0:T(8,128)(2,1)S(1)}) custom-call(s32[32]{0:T(128)} %order_hbm.1, s32[4]{0:T(128)} %spans_hbm.1, bf16[256,512]{1,0:T(8,128)(2,1)} %q_hbm.1, bf16[256,128]{1,0:T(8,128)(2,1)} %k_hbm.1, bf16[256,128]{1,0:T(8,128)(2,1)} %v_hbm.1, ...), custom_call_target="tpu_custom_call" | custom-call | tf_op jit(solution)/shard_map/layer/pallas_call | solution.py:480
  44.4 0.9 %finish.1 = (bf16[256,1024]{1,0:T(8,128)(2,1)}, bf16[256,512]{1,0:T(8,128)(2,1)}, bf16[256,128]{1,0:T(8,128)(2,1)}, bf16[256,128]{1,0:T(8,128)(2,1)}) custom-call(bf16[256,1024]{1,0:T(8,128)(2,1)S(1)} %get-tuple-element.8.refs_0_, bf16[256,512]{1,0:T(8,128)(2,1)S(1)} %get-tuple-element.9.refs_1_, bf16[256,128]{1,0:T(8,128)(2,1)S(1)} %get-tuple-element.10.refs_2_, ...), custom_call_target="tpu_custom_call" | custom-call | tf_op jit(solution)/shard_map/finish/pallas_call | solution.py:535
